TPU v7x, 32 devices: a whole 2x2x4 slice. The times are simulated.
32 devices in a mesh: grp: 2 (over y), row: 8 (over z, x), col: 2 (over core).
Axes of the slice: x: 2, y: 2, z: 4, core: 2. Of those that a mesh axis runs over, the one named last changes fastest.
Arguments:
- normed_features: bfloat16 [64, 32, 256], P(('grp', 'col'), 'row'), parts along dimension 0, may hold values from -6 to 6
- alignment_mask: int32 [64, 32], P(('grp', 'col'), 'row'), parts along dimension 0, may hold values from 0 to 1, as said below
- residue_present_mask: int32 [64], P(('grp', 'row')), parts along dimension 0, may hold values from 0 to 1
- first_factor_matrix: bfloat16 [256, 32], replicated, may hold values from -0.375 to 0.375
- second_factor_matrix: bfloat16 [256, 32], replicated, may hold values from -0.375 to 0.375
- output_weight: bfloat16 [1024, 128], replicated, may hold values from -0.75 to 0.75
- pairwise_bias: float32 [128], replicated, may hold values from -3 to 3
- cotangent: bfloat16 [64, 32, 128], P(('grp', 'row'), 'col'), parts along dimension 0, may hold values from -0.72 to 0.72
Outputs:
- pair_update: bfloat16 [64, 32, 128], P(('grp', 'row'), 'col'), parts along dimension 0
- left_grad: float32 [64, 32, 32], P(('grp', 'col'), 'row'), parts along dimension 0
- right_grad: float32 [64, 32, 32], P(('grp', 'col'), 'row'), parts along dimension 0
There are 2 independent parts, one for each index of `grp`. A program takes and returns all parts, laid end to end along the dimension named above; an argument that names none is the same for every part. Nothing has to cross between parts.
Inputs may be any that keep to these rules, and one draw needn't show every extreme that they name: `alignment_mask`: 0 or 1; sequence 0 (the query) is present at every residue.
All inputs are finite; a program needn't handle non-finite values.
Results may differ from a plain program's by a relative error of at most 0.006.
Values may be sent and summed in bfloat16 or wider, within the bound.
A program may use at most 64 MiB of HBM per device.

v0:
```python
import functools

import jax
import jax.numpy as jnp
from jax import lax
from jax.experimental import pallas as pl
from jax.experimental.pallas import tpu as pltpu
from jax.sharding import PartitionSpec as P

F32 = jnp.float32
BF16 = jnp.bfloat16
MESH = pl.DeviceIdType.MESH
UNROLL = 8
GRANT = 24 << 20


def iota(shape, axis):
    return lax.broadcasted_iota(jnp.int32, shape, axis)


def mm(a, b):
    return lax.dot_general(a, b, (((1,), (0,)), ((), ())), preferred_element_type=F32)


def each(n, f):
    if n <= UNROLL:
        for k in range(n):
            f(k)
    else:

        @pl.loop(0, n)
        def _(k):
            f(k)


def kernel(
    nrow,
    x_hbm, am_hbm, rm_hbm, wl_hbm, wr_hbm, w_hbm, bias_hbm, cot_hbm,
    pu_ref, lg_ref, rg_ref,
    x_ref, am_ref, rm_ref, wl_ref, wr_ref, w_ref, bias_ref, cot_ref,
    g_s, gp_r, f_s, l_r, r_r, ro_r, ct_s, ct_r, cf_r, m_s, m_r,
    w32, a32, b32, o32, c32, p2, q2,
    ssem, rsem, psem, isem,
):
    seq, loc, feat = x_ref.shape
    proj = wl_ref.shape[0]
    half_res, chan = cot_ref.shape[1], cot_ref.shape[2]
    res = nrow * loc
    per_half = half_res // loc
    tiles = proj * seq // 128
    rows = loc * seq
    lo = loc.bit_length() - 1
    sq = seq.bit_length() - 1
    tl = tiles.bit_length() - 1

    grp, row, col = lax.axis_index("grp"), lax.axis_index("row"), lax.axis_index("col")
    other = 1 - col

    def half_of(r):
        return jnp.where(r >= per_half, 1, 0)

    def dev(r, c):
        return (grp, r, c)

    barrier = pltpu.get_barrier_semaphore()

    def greet(k):
        r = lax.rem(row + k, nrow)
        pl.semaphore_signal(barrier, inc=1, device_id=dev(r, other), device_id_type=MESH)
        if isinstance(k, int):
            if k:
                pl.semaphore_signal(barrier, inc=1, device_id=dev(r, col), device_id_type=MESH)
        else:

            @pl.when(k != 0)
            def _():
                pl.semaphore_signal(barrier, inc=1, device_id=dev(r, col), device_id_type=MESH)

    each(nrow, greet)
    loads = [
        pltpu.make_async_copy(src, dst, isem.at[k])
        for k, (src, dst) in enumerate(
            (
                (x_hbm, x_ref), (wl_hbm, wl_ref), (wr_hbm, wr_ref), (am_hbm, am_ref),
                (rm_hbm, rm_ref), (cot_hbm, cot_ref), (w_hbm, w_ref), (bias_hbm, bias_ref),
            )
        )
    ]
    for load in loads:
        load.start()
    for load in loads[:6]:
        load.wait()

    xf = x_ref[...].astype(F32)
    x = jnp.concatenate([xf[:, r, :] for r in range(loc)], axis=0).astype(BF16)
    live = jnp.concatenate(
        [
            jnp.broadcast_to(
                (am_ref[r : r + 1, :] * rm_ref[:, r : r + 1]).astype(F32), (seq, seq)
            )
            for r in range(loc)
        ],
        axis=0,
    )
    diagonal = (iota((rows, seq), 0) & (seq - 1)) == iota((rows, seq), 1)
    live = jnp.sum(jnp.where(diagonal, live, 0.0), axis=1, keepdims=True)
    live = jnp.broadcast_to(live, (rows, 128))
    factors = jnp.concatenate(
        [wl_ref[...], wr_ref[...], jnp.zeros((128 - 2 * proj, feat), BF16)], axis=0
    )
    both = lax.dot_general(x, factors, (((1,), (1,)), ((), ())), preferred_element_type=F32)
    both = jnp.where(iota((rows, 128), 1) < 2 * proj, both, 1.0) * live
    g = both.astype(BF16)
    g_s[...] = g
    lane = iota((rows, 128), 1)
    at = iota((rows, 128), 0)
    m_s[...] = jnp.sum(jnp.where(lane == at, live, 0.0), axis=0, keepdims=True)
    width = 2 * proj * seq
    spread = (iota((128, width), 0) == (iota((128, width), 1) >> sq)).astype(BF16)
    own_seq = (iota((rows, width), 0) & (seq - 1)) == (iota((rows, width), 1) & (seq - 1))
    h = jnp.where(own_seq, mm(g, spread), 0.0).astype(BF16)
    h = jnp.concatenate([h[:, k * 128 : (k + 1) * 128] for k in range(2 * tiles)], axis=0)
    frows, deep = 2 * loc * tiles, 2 * tiles * rows
    fi, ki = iota((frows, deep), 0), iota((frows, deep), 1)
    f_x, f_r, f_t = fi >> (lo + tl), (fi >> tl) & (loc - 1), fi & (tiles - 1)
    k_x, k_t, k_r = ki >> (tl + lo + sq), (ki >> (lo + sq)) & (tiles - 1), (ki >> sq) & (loc - 1)
    pick = ((f_x == k_x) & (f_r == k_r) & (f_t == k_t)).astype(BF16)
    f = mm(pick, h).astype(BF16)
    fr = loc * tiles
    f_s[0] = f[:fr]
    f_s[1] = f[fr:]
    cot32 = cot_ref[...].astype(F32)
    for q in range(per_half if per_half <= UNROLL else 0):
        ct_s[q] = jnp.concatenate(
            [cot32[i, q * loc : (q + 1) * loc, :] for i in range(loc)], axis=0
        ).astype(BF16)
    if per_half > UNROLL:
        c32_rows = c32.shape[0] // loc

        for i in range(loc):
            c32[i * c32_rows : i * c32_rows + half_res] = cot32[i]

        @pl.loop(0, per_half)
        def _(q):
            ct_s[q] = jnp.concatenate(
                [
                    c32[pl.ds(i * c32_rows + q * loc, loc), :]
                    for i in range(loc)
                ],
                axis=0,
            ).astype(BF16)

    pl.semaphore_wait(barrier, 2 * nrow - 1)

    def copy(src, dst, kind, s_slot, r_slot, to):
        return pltpu.make_async_remote_copy(
            src_ref=src, dst_ref=dst, send_sem=ssem.at[kind, s_slot],
            recv_sem=rsem.at[kind, r_slot], device_id=to, device_id_type=MESH,
        )

    def partner(k):
        if k == 0:
            src, dst = g_s, gp_r
        else:
            src, dst = cot_ref, cf_r.at[:, pl.ds(pl.multiple_of(col * half_res, half_res), half_res), :]
        return pltpu.make_async_remote_copy(
            src_ref=src, dst_ref=dst, send_sem=psem.at[k], recv_sem=psem.at[2 + k],
            device_id=dev(row, other), device_id_type=MESH,
        )

    def on(pred, f):
        pl.when(pred)(f)

    def sends(k, act):
        r = lax.rem(row + k, nrow)
        q = jnp.where(r >= per_half, r - per_half, r)
        far = half_of(r) == col

        def same():
            act(copy(f_s.at[1], r_r.at[row], 1, r, row, dev(r, col)))
            act(copy(f_s.at[0], l_r.at[row], 0, r, row, dev(r, col)))
            act(copy(m_s, m_r.at[0, row], 4, r, row, dev(r, col)))
            on(far, lambda: act(copy(ct_s.at[q], ct_r.at[row], 3, r, row, dev(r, col))))

        if isinstance(k, int):
            if k:
                same()
        else:
            on(k != 0, same)
        on(
            half_of(row) == other,
            lambda: act(copy(f_s.at[1], ro_r.at[row], 2, r, row, dev(r, other))),
        )
        act(copy(m_s, m_r.at[1, row], 5, r, row, dev(r, other)))
        on(far, lambda: act(copy(ct_s.at[q], ct_r.at[row], 6, r, row, dev(r, other))))

    partner(0).start()
    partner(1).start()
    each(nrow, lambda j: sends(nrow - 1 - j, lambda d: d.start()))

    l_r[row] = f[:fr]
    r_r[row] = f[fr:]
    m_r[0, row] = m_s[...]
    cf_r[:, pl.ds(pl.multiple_of(col * half_res, half_res), half_res), :] = cot_ref[...]

    @pl.when(half_of(row) == col)
    def _():
        ct_r[row] = ct_s[jnp.where(row >= per_half, row - per_half, row)]

    loads[6].wait()
    loads[7].wait()
    w32[...] = w_ref[...].astype(F32)
    w_c = jnp.concatenate(
        [w32[pl.ds(e, proj, stride=proj), :] for e in range(proj)], axis=1
    ).astype(BF16)
    w_e = jnp.concatenate(
        [w_ref[c * proj : (c + 1) * proj, :] for c in range(proj)], axis=1
    )

    def spread_left(gl, part):
        p = mm(gl[:, :proj], w_c).astype(BF16)
        for e in range(proj):
            for i in range(loc):
                p2[part * proj * seq + e * seq : part * proj * seq + (e + 1) * seq,
                   i * chan : (i + 1) * chan] = p[
                    i * seq : (i + 1) * seq, e * chan : (e + 1) * chan
                ]

    spread_left(g, 0)
    partner(0).wait_recv()
    gp = gp_r[...]
    spread_left(gp, 1)

    def arrivals(k):
        r = lax.rem(row + nrow - k, nrow)

        def same():
            copy(f_s.at[1], r_r.at[r], 1, r, r, dev(r, col)).wait_recv()
            copy(f_s.at[0], l_r.at[r], 0, r, r, dev(r, col)).wait_recv()
            copy(m_s, m_r.at[0, r], 4, r, r, dev(r, col)).wait_recv()
            on(
                half_of(row) == col,
                lambda: copy(ct_s.at[0], ct_r.at[r], 3, r, r, dev(r, col)).wait_recv(),
            )

        if isinstance(k, int):
            if k:
                same()
        else:
            on(k != 0, same)
        on(
            half_of(r) == col,
            lambda: copy(f_s.at[1], ro_r.at[r], 2, r, r, dev(r, other)).wait_recv(),
        )
        copy(m_s, m_r.at[1, r], 5, r, r, dev(r, other)).wait_recv()
        on(
            half_of(row) == other,
            lambda: copy(ct_s.at[0], ct_r.at[r], 6, r, r, dev(r, other)).wait_recv(),
        )

    partner(1).wait_recv()
    each(nrow, arrivals)

    rep = (iota((res, nrow), 0) >> lo == iota((res, nrow), 1)).astype(BF16)
    own_lane = (iota((res, 128), 0) & (loc - 1)) == (iota((res, 128), 1) >> sq)
    z = [
        jnp.where(own_lane, mm(rep, m_r[k].reshape(nrow, 128).astype(BF16)), 0.0).astype(BF16)
        for k in range(2)
    ]
    counts = []
    for b in range(loc):
        total = None
        for k, gl in enumerate((g, gp)):
            m_b = jnp.broadcast_to(
                gl[b * seq : (b + 1) * seq, 2 * proj : 2 * proj + 1].astype(F32), (seq, 128)
            ).astype(BF16)
            term = mm(z[k], jnp.concatenate([m_b] * (128 // seq), axis=0))
            total = term if total is None else total + term
        counts.append(jnp.maximum(total, 1.0))

    def unflatten(ref, n, start=0):
        return jnp.concatenate(
            [ref[pl.ds(start + t, n, stride=tiles), :] for t in range(tiles)], axis=1
        ).astype(BF16)

    a32[...] = r_r[...].astype(F32).reshape(res * tiles, 128)
    b32[...] = l_r[...].astype(F32).reshape(res * tiles, 128)
    c32[...] = ct_r[...].astype(F32).reshape(res * loc, 128)
    o32[...] = (
        ro_r[pl.ds(col * per_half, per_half)].astype(F32).reshape(half_res * tiles, 128)
    )
    right_all = unflatten(a32, res)
    left_all = unflatten(b32, res)

    start = pl.multiple_of(col * half_res * tiles, half_res * tiles)
    r_half = jnp.concatenate(
        [unflatten(a32, half_res, start), unflatten(o32, half_res)], axis=1
    )
    mapped = mm(r_half, p2[...])
    bias = bias_ref[...]
    for i in range(loc):
        w32[:res] = counts[i]
        div = w32[pl.ds(pl.multiple_of(col * half_res, half_res), half_res), :]
        pu_ref[i] = (mapped[:, i * chan : (i + 1) * chan] / div + bias).astype(BF16)

    def grad(flat, scaled, weight):
        q = lax.dot_general(
            flat, scaled, (((0,), (0,)), ((), ())), preferred_element_type=F32
        ).astype(BF16)
        for e in range(proj):
            for i in range(loc):
                q2[i * seq : (i + 1) * seq, e * chan : (e + 1) * chan] = q[
                    e * seq : (e + 1) * seq, i * chan : (i + 1) * chan
                ]
        return lax.dot_general(
            q2[...], weight, (((1,), (1,)), ((), ())), preferred_element_type=F32
        )

    scaled = jnp.concatenate(
        [(cf_r[i].astype(F32) / counts[i]).astype(BF16) for i in range(loc)], axis=1
    )
    lg_ref[...] = grad(right_all, scaled, w_c)
    scaled_t = jnp.concatenate(
        [
            (c32[pl.ds(j, res, stride=loc), :] / counts[j]).astype(BF16)
            for j in range(loc)
        ],
        axis=1,
    )
    rg_ref[...] = grad(left_all, scaled_t, w_e)

    partner(0).wait_send()
    partner(1).wait_send()
    each(nrow, lambda j: sends(nrow - 1 - j, lambda d: d.wait_send()))


def finish(pu_in, lg_in, rg_in, pu_ref, lg_ref, rg_ref):
    seq, loc, _ = lg_ref.shape
    pu_ref[...] = pu_in[...]
    for i in range(loc):
        lg_ref[:, i, :] = lg_in[i * seq : (i + 1) * seq, :]
        rg_ref[:, i, :] = rg_in[i * seq : (i + 1) * seq, :]


def per_device(nrow, x, am, rm, wl, wr, w, bias, cot):
    seq, loc, _ = x.shape
    proj = wl.shape[1]
    half_res, chan = cot.shape[1], cot.shape[2]
    res = nrow * loc
    tiles = proj * seq // 128
    fr = loc * tiles
    rows = loc * seq
    hbm = pl.BlockSpec(memory_space=pltpu.HBM)
    vm = pl.BlockSpec(memory_space=pltpu.VMEM)
    operands = (x, am.T, rm.reshape(1, loc), wl.T, wr.T, w, bias.reshape(1, chan), cot)
    held = [pltpu.with_memory_space_constraint(a, pltpu.HBM) for a in operands]
    pu, lg, rg = pl.pallas_call(
        functools.partial(kernel, nrow),
        out_shape=(
            jax.ShapeDtypeStruct(cot.shape, BF16),
            jax.ShapeDtypeStruct((rows, proj), F32),
            jax.ShapeDtypeStruct((rows, proj), F32),
        ),
        in_specs=[hbm] * 8,
        out_specs=(vm, vm, vm),
        scratch_shapes=[pltpu.VMEM(a.shape, a.dtype) for a in operands]
        + [
            pltpu.VMEM((rows, 128), BF16),
            pltpu.VMEM((rows, 128), BF16),
            pltpu.VMEM((2, fr, 128), BF16),
            pltpu.VMEM((nrow, fr, 128), BF16),
            pltpu.VMEM((nrow, fr, 128), BF16),
            pltpu.VMEM((nrow, fr, 128), BF16),
            pltpu.VMEM((half_res // loc, loc * loc, 128), BF16),
            pltpu.VMEM((nrow, loc * loc, 128), BF16),
            pltpu.VMEM((loc, res, chan), BF16),
            pltpu.VMEM((1, 128), F32),
            pltpu.VMEM((2, nrow, 1, 128), F32),
            pltpu.VMEM((max(proj * proj, res), chan), F32),
            pltpu.VMEM((res * tiles, 128), F32),
            pltpu.VMEM((res * tiles, 128), F32),
            pltpu.VMEM((half_res * tiles, 128), F32),
            pltpu.VMEM((res * loc, 128), F32),
            pltpu.VMEM((2 * proj * seq, loc * chan), BF16),
            pltpu.VMEM((rows, proj * chan), BF16),
            pltpu.SemaphoreType.DMA((7, nrow)),
            pltpu.SemaphoreType.DMA((7, nrow)),
            pltpu.SemaphoreType.DMA((4,)),
            pltpu.SemaphoreType.DMA((8,)),
        ],
        compiler_params=pltpu.CompilerParams(
            collective_id=0, has_side_effects=True, vmem_limit_bytes=GRANT
        ),
    )(*held)
    grads = jax.ShapeDtypeStruct((seq, loc, proj), F32)
    return pl.pallas_call(
        finish,
        out_shape=(jax.ShapeDtypeStruct(cot.shape, BF16), grads, grads),
        in_specs=[vm] * 3,
        out_specs=(vm, vm, vm),
        compiler_params=pltpu.CompilerParams(vmem_limit_bytes=GRANT),
    )(pu, lg, rg)


def solution(mesh):
    placed = (
        P(("grp", "col"), "row", None),
        P(("grp", "col"), "row"),
        P(("grp", "row")),
        P(),
        P(),
        P(),
        P(),
        P(("grp", "row"), "col", None),
    )
    return jax.shard_map(
        functools.partial(per_device, mesh.shape["row"]),
        mesh=mesh,
        in_specs=placed,
        out_specs=(
            P(("grp", "row"), "col", None),
            P(("grp", "col"), "row", None),
            P(("grp", "col"), "row", None),
        ),
        check_vma=False,
    )
```

profile of v0, /device:TPU:0, one launch (start us, length us, event | category | flops | bytes accessed | tf_op | source)
XLA Modules:
  0.0 14.2 jit_solution(510204011663067821)
XLA Ops:
  0.6 12.9 %shard_map.103 = (bf16[4,16,128]{2,1,0:T(8,128)(2,1)S(1)}, f32[64,32]{1,0:T(8,128)S(1)}, f32[64,32]{1,0:T(8,128)S(1)}) custom-call(bf16[16,4,256]{2,1,0:T(4,128)(2,1)} %x_hbm.1, s32[4,16]{1,0:T(4,128)} %bitcast.7, s32[1,4]{1,0:T(1,128)} %bitcast.8, bf16[32,256]{1,0:T(8,128)(2,1)} %bitcast.5, bf16[32,256]{1,0:T(8,128)(2,1)} %bitcast.6, ...), custom_call_target="tpu_custom_call" | custom-call | tf_op jit(solution)/shard_map/pallas_call | solution.py:357
  13.6 0.7 %shard_map.104 = (bf16[4,16,128]{2,1,0:T(8,128)(2,1)}, f32[16,4,32]{2,1,0:T(4,128)}, f32[16,4,32]{2,1,0:T(4,128)}) custom-call(bf16[4,16,128]{2,1,0:T(8,128)(2,1)S(1)} %get-tuple-element.6.pu_in, f32[64,32]{1,0:T(8,128)S(1)} %get-tuple-element.7.lg_in, f32[64,32]{1,0:T(8,128)S(1)} %get-tuple-element.8.rg_in), custom_call_target="tpu_custom_call" | custom-call | tf_op jit(solution)/shard_map/pallas_call | solution.py:396
where the time goes:
time: 14.4 us; the launch traced here: 14.2 us
  Pallas kernels  13.6 us (94%)
  between operations  0.64 us (4%)
    pallas_call x1, Pallas kernels, per_device(): pl.pallas_call(functools.partial(kernel, nrow), out_shape=(jax.ShapeDtype...  12.9 us
    pallas_call x1, Pallas kernels, per_device(): pl.pallas_call(finish, out_shape=(jax.ShapeDtypeStruct(cot.shape, BF16),...  0.66 us

commit v1 on v0

--- a/solution.py
+++ b/solution.py
@@ -64,8 +64,18 @@
 
     barrier = pltpu.get_barrier_semaphore()
 
-    def greet(k):
-        r = lax.rem(row + k, nrow)
+    def peer(k):
+        if nrow & (nrow - 1):
+            return lax.rem(row + k, nrow)
+        r = 0
+        for b in range(nrow.bit_length() - 1):
+            bit = lax.rem(lax.div(row, 1 << b) + k // (1 << b), 2)
+            r = r + bit * (1 << b)
+        return r
+
+    def greet(j):
+        k = nrow - 1 - j
+        r = peer(k)
         pl.semaphore_signal(barrier, inc=1, device_id=dev(r, other), device_id_type=MESH)
         if isinstance(k, int):
             if k:
@@ -171,32 +181,38 @@
     def on(pred, f):
         pl.when(pred)(f)
 
-    def sends(k, act):
-        r = lax.rem(row + k, nrow)
+    def sends(k, phase, act):
+        r = peer(k)
         q = jnp.where(r >= per_half, r - per_half, r)
         far = half_of(r) == col
 
         def same():
-            act(copy(f_s.at[1], r_r.at[row], 1, r, row, dev(r, col)))
-            act(copy(f_s.at[0], l_r.at[row], 0, r, row, dev(r, col)))
-            act(copy(m_s, m_r.at[0, row], 4, r, row, dev(r, col)))
-            on(far, lambda: act(copy(ct_s.at[q], ct_r.at[row], 3, r, row, dev(r, col))))
+            if phase == 0:
+                act(copy(m_s, m_r.at[0, row], 4, r, row, dev(r, col)))
+                on(far, lambda: act(copy(ct_s.at[q], ct_r.at[row], 3, r, row, dev(r, col))))
+            elif phase == 1:
+                act(copy(f_s.at[1], r_r.at[row], 1, r, row, dev(r, col)))
+            else:
+                act(copy(f_s.at[0], l_r.at[row], 0, r, row, dev(r, col)))
 
         if isinstance(k, int):
             if k:
                 same()
         else:
             on(k != 0, same)
-        on(
-            half_of(row) == other,
-            lambda: act(copy(f_s.at[1], ro_r.at[row], 2, r, row, dev(r, other))),
-        )
-        act(copy(m_s, m_r.at[1, row], 5, r, row, dev(r, other)))
-        on(far, lambda: act(copy(ct_s.at[q], ct_r.at[row], 6, r, row, dev(r, other))))
+        if phase == 0:
+            act(copy(m_s, m_r.at[1, row], 5, r, row, dev(r, other)))
+            on(far, lambda: act(copy(ct_s.at[q], ct_r.at[row], 6, r, row, dev(r, other))))
+        elif phase == 1:
+            on(
+                half_of(row) == other,
+                lambda: act(copy(f_s.at[1], ro_r.at[row], 2, r, row, dev(r, other))),
+            )
 
     partner(0).start()
     partner(1).start()
-    each(nrow, lambda j: sends(nrow - 1 - j, lambda d: d.start()))
+    for phase in range(3):
+        each(nrow, lambda j: sends(nrow - 1 - j, phase, lambda d: d.start()))
 
     l_r[row] = f[:fr]
     r_r[row] = f[fr:]
@@ -209,7 +225,7 @@
 
     loads[6].wait()
     loads[7].wait()
-    w32[...] = w_ref[...].astype(F32)
+    w32[: proj * proj] = w_ref[...].astype(F32)
     w_c = jnp.concatenate(
         [w32[pl.ds(e, proj, stride=proj), :] for e in range(proj)], axis=1
     ).astype(BF16)
@@ -231,35 +247,40 @@
     gp = gp_r[...]
     spread_left(gp, 1)
 
-    def arrivals(k):
-        r = lax.rem(row + nrow - k, nrow)
+    def arrivals(k, phase):
+        r = peer(k)
 
         def same():
-            copy(f_s.at[1], r_r.at[r], 1, r, r, dev(r, col)).wait_recv()
-            copy(f_s.at[0], l_r.at[r], 0, r, r, dev(r, col)).wait_recv()
-            copy(m_s, m_r.at[0, r], 4, r, r, dev(r, col)).wait_recv()
-            on(
-                half_of(row) == col,
-                lambda: copy(ct_s.at[0], ct_r.at[r], 3, r, r, dev(r, col)).wait_recv(),
-            )
+            if phase == 0:
+                copy(m_s, m_r.at[0, r], 4, r, r, dev(r, col)).wait_recv()
+                on(
+                    half_of(row) == col,
+                    lambda: copy(ct_s.at[0], ct_r.at[r], 3, r, r, dev(r, col)).wait_recv(),
+                )
+            elif phase == 1:
+                copy(f_s.at[1], r_r.at[r], 1, r, r, dev(r, col)).wait_recv()
+            else:
+                copy(f_s.at[0], l_r.at[r], 0, r, r, dev(r, col)).wait_recv()
 
         if isinstance(k, int):
             if k:
                 same()
         else:
             on(k != 0, same)
-        on(
-            half_of(r) == col,
-            lambda: copy(f_s.at[1], ro_r.at[r], 2, r, r, dev(r, other)).wait_recv(),
-        )
-        copy(m_s, m_r.at[1, r], 5, r, r, dev(r, other)).wait_recv()
-        on(
-            half_of(row) == other,
-            lambda: copy(ct_s.at[0], ct_r.at[r], 6, r, r, dev(r, other)).wait_recv(),
-        )
+        if phase == 0:
+            copy(m_s, m_r.at[1, r], 5, r, r, dev(r, other)).wait_recv()
+            on(
+                half_of(row) == other,
+                lambda: copy(ct_s.at[0], ct_r.at[r], 6, r, r, dev(r, other)).wait_recv(),
+            )
+        elif phase == 1:
+            on(
+                half_of(r) == col,
+                lambda: copy(f_s.at[1], ro_r.at[r], 2, r, r, dev(r, other)).wait_recv(),
+            )
 
     partner(1).wait_recv()
-    each(nrow, arrivals)
+    each(nrow, lambda k: arrivals(k, 0))
 
     rep = (iota((res, nrow), 0) >> lo == iota((res, nrow), 1)).astype(BF16)
     own_lane = (iota((res, 128), 0) & (loc - 1)) == (iota((res, 128), 1) >> sq)
@@ -283,15 +304,26 @@
             [ref[pl.ds(start + t, n, stride=tiles), :] for t in range(tiles)], axis=1
         ).astype(BF16)
 
+    c32[...] = ct_r[...].astype(F32).reshape(res * loc, 128)
+    scaled = jnp.concatenate(
+        [(cf_r[i].astype(F32) / counts[i]).astype(BF16) for i in range(loc)], axis=1
+    )
+    scaled_t = jnp.concatenate(
+        [
+            (c32[pl.ds(j, res, stride=loc), :] / counts[j]).astype(BF16)
+            for j in range(loc)
+        ],
+        axis=1,
+    )
+    for i in range(loc):
+        w32[i * res : (i + 1) * res] = 1.0 / counts[i]
+
+    each(nrow, lambda k: arrivals(k, 1))
     a32[...] = r_r[...].astype(F32).reshape(res * tiles, 128)
-    b32[...] = l_r[...].astype(F32).reshape(res * tiles, 128)
-    c32[...] = ct_r[...].astype(F32).reshape(res * loc, 128)
     o32[...] = (
         ro_r[pl.ds(col * per_half, per_half)].astype(F32).reshape(half_res * tiles, 128)
     )
     right_all = unflatten(a32, res)
-    left_all = unflatten(b32, res)
-
     start = pl.multiple_of(col * half_res * tiles, half_res * tiles)
     r_half = jnp.concatenate(
         [unflatten(a32, half_res, start), unflatten(o32, half_res)], axis=1
@@ -299,9 +331,8 @@
     mapped = mm(r_half, p2[...])
     bias = bias_ref[...]
     for i in range(loc):
-        w32[:res] = counts[i]
-        div = w32[pl.ds(pl.multiple_of(col * half_res, half_res), half_res), :]
-        pu_ref[i] = (mapped[:, i * chan : (i + 1) * chan] / div + bias).astype(BF16)
+        inverse = w32[pl.ds(pl.multiple_of(i * res + col * half_res, half_res), half_res), :]
+        pu_ref[i] = (mapped[:, i * chan : (i + 1) * chan] * inverse + bias).astype(BF16)
 
     def grad(flat, scaled, weight):
         q = lax.dot_general(
@@ -316,22 +347,15 @@
             q2[...], weight, (((1,), (1,)), ((), ())), preferred_element_type=F32
         )
 
-    scaled = jnp.concatenate(
-        [(cf_r[i].astype(F32) / counts[i]).astype(BF16) for i in range(loc)], axis=1
-    )
     lg_ref[...] = grad(right_all, scaled, w_c)
-    scaled_t = jnp.concatenate(
-        [
-            (c32[pl.ds(j, res, stride=loc), :] / counts[j]).astype(BF16)
-            for j in range(loc)
-        ],
-        axis=1,
-    )
-    rg_ref[...] = grad(left_all, scaled_t, w_e)
+    each(nrow, lambda k: arrivals(k, 2))
+    b32[...] = l_r[...].astype(F32).reshape(res * tiles, 128)
+    rg_ref[...] = grad(unflatten(b32, res), scaled_t, w_e)
 
     partner(0).wait_send()
     partner(1).wait_send()
-    each(nrow, lambda j: sends(nrow - 1 - j, lambda d: d.wait_send()))
+    for phase in range(3):
+        each(nrow, lambda j: sends(nrow - 1 - j, phase, lambda d: d.wait_send()))
 
 
 def finish(pu_in, lg_in, rg_in, pu_ref, lg_ref, rg_ref):
@@ -376,7 +400,7 @@
             pltpu.VMEM((loc, res, chan), BF16),
             pltpu.VMEM((1, 128), F32),
             pltpu.VMEM((2, nrow, 1, 128), F32),
-            pltpu.VMEM((max(proj * proj, res), chan), F32),
+            pltpu.VMEM((max(proj * proj, loc * res), chan), F32),
             pltpu.VMEM((res * tiles, 128), F32),
             pltpu.VMEM((res * tiles, 128), F32),
             pltpu.VMEM((half_res * tiles, 128), F32),

time: 14.4 us -> 14.3 us (level)
  no operation moved by 1% of the time
where the time goes in v1:
time: 14.3 us; the launch traced here: 14.1 us
  Pallas kernels  13.5 us (94%)
  between operations  0.64 us (4%)
    pallas_call x1, Pallas kernels, per_device(): pl.pallas_call(functools.partial(kernel, nrow), out_shape=(jax.ShapeDtype...  12.8 us
    pallas_call x1, Pallas kernels, per_device(): pl.pallas_call(finish, out_shape=(jax.ShapeDtypeStruct(cot.shape, BF16),...  0.66 us

profile of v1, /device:TPU:0, one launch (start us, length us, event | category | flops | bytes accessed | tf_op | source)
XLA Modules:
  0.0 14.1 jit_solution(7192714469616784830)
XLA Ops:
  0.6 12.8 %shard_map.103 = (bf16[4,16,128]{2,1,0:T(8,128)(2,1)S(1)}, f32[64,32]{1,0:T(8,128)S(1)}, f32[64,32]{1,0:T(8,128)S(1)}) custom-call(bf16[16,4,256]{2,1,0:T(4,128)(2,1)} %x_hbm.1, s32[4,16]{1,0:T(4,128)} %bitcast.7, s32[1,4]{1,0:T(1,128)} %bitcast.8, bf16[32,256]{1,0:T(8,128)(2,1)} %bitcast.5, bf16[32,256]{1,0:T(8,128)(2,1)} %bitcast.6, ...), custom_call_target="tpu_custom_call" | custom-call | tf_op jit(solution)/shard_map/pallas_call | solution.py:381
  13.5 0.7 %shard_map.104 = (bf16[4,16,128]{2,1,0:T(8,128)(2,1)}, f32[16,4,32]{2,1,0:T(4,128)}, f32[16,4,32]{2,1,0:T(4,128)}) custom-call(bf16[4,16,128]{2,1,0:T(8,128)(2,1)S(1)} %get-tuple-element.6.pu_in, f32[64,32]{1,0:T(8,128)S(1)} %get-tuple-element.7.lg_in, f32[64,32]{1,0:T(8,128)S(1)} %get-tuple-element.8.rg_in), custom_call_target="tpu_custom_call" | custom-call | tf_op jit(solution)/shard_map/pallas_call | solution.py:420

commit v2 on v1

--- a/solution.py
+++ b/solution.py
@@ -191,9 +191,9 @@
                 act(copy(m_s, m_r.at[0, row], 4, r, row, dev(r, col)))
                 on(far, lambda: act(copy(ct_s.at[q], ct_r.at[row], 3, r, row, dev(r, col))))
             elif phase == 1:
+                act(copy(f_s.at[0], l_r.at[row], 0, r, row, dev(r, col)))
+            elif phase == 2:
                 act(copy(f_s.at[1], r_r.at[row], 1, r, row, dev(r, col)))
-            else:
-                act(copy(f_s.at[0], l_r.at[row], 0, r, row, dev(r, col)))
 
         if isinstance(k, int):
             if k:
@@ -203,7 +203,7 @@
         if phase == 0:
             act(copy(m_s, m_r.at[1, row], 5, r, row, dev(r, other)))
             on(far, lambda: act(copy(ct_s.at[q], ct_r.at[row], 6, r, row, dev(r, other))))
-        elif phase == 1:
+        elif phase == 3:
             on(
                 half_of(row) == other,
                 lambda: act(copy(f_s.at[1], ro_r.at[row], 2, r, row, dev(r, other))),
@@ -211,7 +211,7 @@
 
     partner(0).start()
     partner(1).start()
-    for phase in range(3):
+    for phase in range(4):
         each(nrow, lambda j: sends(nrow - 1 - j, phase, lambda d: d.start()))
 
     l_r[row] = f[:fr]
@@ -258,9 +258,9 @@
                     lambda: copy(ct_s.at[0], ct_r.at[r], 3, r, r, dev(r, col)).wait_recv(),
                 )
             elif phase == 1:
+                copy(f_s.at[0], l_r.at[r], 0, r, r, dev(r, col)).wait_recv()
+            elif phase == 2:
                 copy(f_s.at[1], r_r.at[r], 1, r, r, dev(r, col)).wait_recv()
-            else:
-                copy(f_s.at[0], l_r.at[r], 0, r, r, dev(r, col)).wait_recv()
 
         if isinstance(k, int):
             if k:
@@ -273,7 +273,7 @@
                 half_of(row) == other,
                 lambda: copy(ct_s.at[0], ct_r.at[r], 6, r, r, dev(r, other)).wait_recv(),
             )
-        elif phase == 1:
+        elif phase == 3:
             on(
                 half_of(r) == col,
                 lambda: copy(f_s.at[1], ro_r.at[r], 2, r, r, dev(r, other)).wait_recv(),
@@ -318,22 +318,6 @@
     for i in range(loc):
         w32[i * res : (i + 1) * res] = 1.0 / counts[i]
 
-    each(nrow, lambda k: arrivals(k, 1))
-    a32[...] = r_r[...].astype(F32).reshape(res * tiles, 128)
-    o32[...] = (
-        ro_r[pl.ds(col * per_half, per_half)].astype(F32).reshape(half_res * tiles, 128)
-    )
-    right_all = unflatten(a32, res)
-    start = pl.multiple_of(col * half_res * tiles, half_res * tiles)
-    r_half = jnp.concatenate(
-        [unflatten(a32, half_res, start), unflatten(o32, half_res)], axis=1
-    )
-    mapped = mm(r_half, p2[...])
-    bias = bias_ref[...]
-    for i in range(loc):
-        inverse = w32[pl.ds(pl.multiple_of(i * res + col * half_res, half_res), half_res), :]
-        pu_ref[i] = (mapped[:, i * chan : (i + 1) * chan] * inverse + bias).astype(BF16)
-
     def grad(flat, scaled, weight):
         q = lax.dot_general(
             flat, scaled, (((0,), (0,)), ((), ())), preferred_element_type=F32
@@ -347,14 +331,30 @@
             q2[...], weight, (((1,), (1,)), ((), ())), preferred_element_type=F32
         )
 
-    lg_ref[...] = grad(right_all, scaled, w_c)
-    each(nrow, lambda k: arrivals(k, 2))
+    each(nrow, lambda k: arrivals(k, 1))
     b32[...] = l_r[...].astype(F32).reshape(res * tiles, 128)
     rg_ref[...] = grad(unflatten(b32, res), scaled_t, w_e)
 
+    each(nrow, lambda k: arrivals(k, 2))
+    a32[...] = r_r[...].astype(F32).reshape(res * tiles, 128)
+    lg_ref[...] = grad(unflatten(a32, res), scaled, w_c)
+
+    start = pl.multiple_of(col * half_res * tiles, half_res * tiles)
+    deep = proj * seq
+    mapped = mm(unflatten(a32, half_res, start), p2[:deep])
+    bias = bias_ref[...]
+    each(nrow, lambda k: arrivals(k, 3))
+    o32[...] = (
+        ro_r[pl.ds(col * per_half, per_half)].astype(F32).reshape(half_res * tiles, 128)
+    )
+    mapped = mapped + mm(unflatten(o32, half_res), p2[deep:])
+    for i in range(loc):
+        inverse = w32[pl.ds(pl.multiple_of(i * res + col * half_res, half_res), half_res), :]
+        pu_ref[i] = (mapped[:, i * chan : (i + 1) * chan] * inverse + bias).astype(BF16)
+
     partner(0).wait_send()
     partner(1).wait_send()
-    for phase in range(3):
+    for phase in range(4):
         each(nrow, lambda j: sends(nrow - 1 - j, phase, lambda d: d.wait_send()))
 
 

time: 14.3 us -> 14.4 us (level)
    pallas_call x1, Pallas kernels: 12.8 us -> 13 us  [per_device(): pl.pallas_call(functools.partial(kernel, nrow), out_shape=(jax.ShapeDtype...]
where the time goes in v2:
time: 14.4 us; the launch traced here: 14.3 us
  Pallas kernels  13.6 us (94%)
  between operations  0.64 us (4%)
    pallas_call x1, Pallas kernels, per_device(): pl.pallas_call(functools.partial(kernel, nrow), out_shape=(jax.ShapeDtype...  13 us
    pallas_call x1, Pallas kernels, per_device(): pl.pallas_call(finish, out_shape=(jax.ShapeDtypeStruct(cot.shape, BF16),...  0.66 us

profile of v2, /device:TPU:0, one launch (start us, length us, event | category | flops | bytes accessed | tf_op | source)
XLA Modules:
  0.0 14.3 jit_solution(17691795044853361839)
XLA Ops:
  0.6 13.0 %shard_map.103 = (bf16[4,16,128]{2,1,0:T(8,128)(2,1)S(1)}, f32[64,32]{1,0:T(8,128)S(1)}, f32[64,32]{1,0:T(8,128)S(1)}) custom-call(bf16[16,4,256]{2,1,0:T(4,128)(2,1)} %x_hbm.1, s32[4,16]{1,0:T(4,128)} %bitcast.7, s32[1,4]{1,0:T(1,128)} %bitcast.8, bf16[32,256]{1,0:T(8,128)(2,1)} %bitcast.5, bf16[32,256]{1,0:T(8,128)(2,1)} %bitcast.6, ...), custom_call_target="tpu_custom_call" | custom-call | tf_op jit(solution)/shard_map/pallas_call | solution.py:381
  13.6 0.7 %shard_map.104 = (bf16[4,16,128]{2,1,0:T(8,128)(2,1)}, f32[16,4,32]{2,1,0:T(4,128)}, f32[16,4,32]{2,1,0:T(4,128)}) custom-call(bf16[4,16,128]{2,1,0:T(8,128)(2,1)S(1)} %get-tuple-element.6.pu_in, f32[64,32]{1,0:T(8,128)S(1)} %get-tuple-element.7.lg_in, f32[64,32]{1,0:T(8,128)S(1)} %get-tuple-element.8.rg_in), custom_call_target="tpu_custom_call" | custom-call | tf_op jit(solution)/shard_map/pallas_call | solution.py:420
